TPU v7x, 512 devices: a whole 4x8x8 slice. The times are simulated.
512 devices in a mesh: coil: 32 (over x, y), slab: 16 (over z, core).
Axes of the slice: x: 4, y: 8, z: 8, core: 2. Of those that a mesh axis runs over, the one named last changes fastest.
Arguments:
- adjoint_data: float32 [16, 192, 384], P('slab', 'coil'), may hold values from -80 to 80
- denoised: float32 [16, 192, 384], P('slab', 'coil'), may hold values from -8 to 8, as said below
- sensitivity: float32 [32, 16, 192, 384], P('coil', 'slab'), may hold values from -2 to 2, as said below
- kernel: float32 [16, 384, 384], P(None, 'slab'), may hold values from 0.1 to 2, as said below
- conv_in: bfloat16 [54, 64], replicated, may hold values from -0.875 to 0.875
- conv_mid: bfloat16 [1728, 64], replicated, may hold values from -0.15625 to 0.15625
- conv_out: bfloat16 [1728, 2], replicated, may hold values from -0.15625 to 0.15625
Outputs:
- solution: float32 [16, 192, 384], P('slab', 'coil')
- refined: float32 [16, 192, 384], P('slab', 'coil')
Inputs may be any that keep to these rules, and one draw needn't show every extreme that they name: `denoised`: real and imaginary parts of the previous cascade's image. `sensitivity`: real and imaginary parts of the coil maps. Positive kernel values.
All inputs are finite; a program needn't handle non-finite values.
Results may differ from a plain program's by a relative error of at most 0.0023.
Values may be sent and summed in bfloat16 or wider, within the bound.
A program may use at most 64 MiB of HBM per device.

v0:
```python
import math
import jax
import jax.numpy as jnp
from jax import lax
from jax.sharding import PartitionSpec as P

ITERS = 2
reg_weight = 0.5
highest = lax.Precision.HIGHEST


def with_halo(cells, sides, width):
    for axis, dim in sides:
        count = lax.axis_size(axis)
        ends = count - 1
        head = lax.slice_in_dim(cells, 0, width, axis=dim)
        tail = lax.slice_in_dim(cells, cells.shape[dim] - width, cells.shape[dim], axis=dim)
        cells = jnp.concatenate(
            [
                lax.ppermute(tail, axis, [(i, (i + 1) % count) for i in range(ends)]),
                cells,
                lax.ppermute(head, axis, [((i + 1) % count, i) for i in range(ends)]),
            ],
            axis=dim,
        )
    return cells


def dft_tables(out_len, in_len, length, inverse):
    out_index = lax.broadcasted_iota(jnp.int32, (out_len, in_len), 0)
    in_index = lax.broadcasted_iota(jnp.int32, (out_len, in_len), 1)
    phases = (out_index * in_index % length).astype(jnp.float32) * (2.0 * math.pi / length)
    if inverse:
        return (jnp.cos(phases) / length, jnp.sin(phases) / length)
    return (jnp.cos(phases), -jnp.sin(phases))


def block_matrix(tables):
    cos_table = tables[0]
    sin_table = tables[1]
    upper = jnp.concatenate([cos_table.T, sin_table.T], axis=1)
    lower = jnp.concatenate([-sin_table.T, cos_table.T], axis=1)
    return jnp.concatenate([upper, lower], axis=0)


def along_axis(values, tables, einsum_form):
    half_len = values.shape[-1] // 2
    real_part = jnp.einsum(einsum_form, tables[0], values, precision=highest)
    imag_part = jnp.einsum(einsum_form, tables[1], values, precision=highest)
    return jnp.concatenate(
        [
            real_part[..., :half_len] - imag_part[..., half_len:],
            real_part[..., half_len:] + imag_part[..., :half_len],
        ],
        axis=-1,
    )


def complex_product(factor_one, factor_two):
    half_len = factor_one.shape[-1] // 2
    real_one = factor_one[..., :half_len]
    imag_one = factor_one[..., half_len:]
    real_two = factor_two[..., :half_len]
    imag_two = factor_two[..., half_len:]
    return jnp.concatenate(
        [real_one * real_two - imag_one * imag_two, real_one * imag_two + imag_one * real_two],
        axis=-1,
    )


def conj_product(factor_one, factor_two):
    half_len = factor_one.shape[-1] // 2
    real_one = factor_one[..., :half_len]
    imag_one = factor_one[..., half_len:]
    real_two = factor_two[..., :half_len]
    imag_two = factor_two[..., half_len:]
    return jnp.concatenate(
        [real_one * real_two + imag_one * imag_two, real_one * imag_two - imag_one * real_two],
        axis=-1,
    )


def convolve(features, weights, in_channels):
    padded = with_halo(features, (("coil", 1), ("slab", 0)), 1)
    depth_here = features.shape[0]
    rows_here = features.shape[1]
    side_len = features.shape[2] // in_channels
    padded_cube = padded.reshape(depth_here + 2, rows_here + 2, side_len, in_channels)
    padded_cube = jnp.pad(padded_cube, ((0, 0), (0, 0), (1, 1), (0, 0)))
    width_taps = 9 * in_channels
    running = None
    for shift_z in range(3):
        tap_list = [
            padded_cube[
                shift_z : shift_z + depth_here,
                shift_x : shift_x + rows_here,
                shift_y : shift_y + side_len,
                :,
            ]
            for shift_x in range(3)
            for shift_y in range(3)
        ]
        patches = jnp.concatenate(tap_list, axis=-1).reshape(-1, width_taps)
        partial_sum = jnp.dot(
            patches,
            weights[shift_z * width_taps : (shift_z + 1) * width_taps],
            preferred_element_type=jnp.float32,
        )
        running = partial_sum if shift_z == 0 else running + partial_sum
    return running


def shards(adjoint_data, denoised, sensitivity, kernel, conv_in, conv_mid, conv_out):
    side_len = sensitivity.shape[2]
    depth_len = kernel.shape[0]
    grid_len = kernel.shape[2]
    fwd_plane = dft_tables(grid_len, side_len, grid_len, False)
    inv_plane = dft_tables(side_len, grid_len, grid_len, True)
    fwd_depth = dft_tables(depth_len, depth_len, depth_len, False)
    inv_depth = dft_tables(depth_len, depth_len, depth_len, True)
    fwd_last = block_matrix(fwd_plane)
    inv_last = block_matrix(inv_plane)

    def total_squares(residual):
        return lax.psum(jnp.sum(residual * residual), ("coil", "slab"))

    right_side = adjoint_data + reg_weight * denoised
    solution = jnp.zeros_like(right_side)
    residual = right_side
    direction = right_side
    norm_now = total_squares(residual)
    for iteration in range(ITERS):
        products = complex_product(
            sensitivity, lax.all_gather(direction, "coil", axis=1, tiled=True)[None]
        )
        products = jnp.matmul(products, fwd_last, precision=highest)
        spread = along_axis(products, fwd_plane, "kn,cznw->czkw")
        apply_pencil = lax.all_to_all(spread, "slab", split_axis=2, concat_axis=1, tiled=True)
        spectrum = along_axis(apply_pencil, fwd_depth, "kn,cnxw->ckxw")
        shape_now = spectrum.shape
        split_form = spectrum.reshape(shape_now[0], shape_now[1], shape_now[2], 2, grid_len)
        weighted = split_form * kernel[None, :, :, None, :]
        returned = along_axis(weighted.reshape(shape_now), inv_depth, "kn,cnxw->ckxw")
        slab_back = lax.all_to_all(returned, "slab", split_axis=1, concat_axis=2, tiled=True)
        image_back = along_axis(slab_back, inv_plane, "kn,cznw->czkw")
        image_back = jnp.matmul(image_back, inv_last, precision=highest)
        coil_sum = jnp.sum(conj_product(sensitivity, image_back), axis=0)
        summed = lax.psum_scatter(coil_sum, "coil", scatter_dimension=1, tiled=True)
        image_out = summed + reg_weight * direction
        local_curv = jnp.sum(direction * image_out)
        image_out, local_curv = (image_out, local_curv)
        curvature = lax.psum(local_curv, ("coil", "slab"))
        step_size = norm_now / curvature
        solution = solution + step_size * direction
        if iteration + 1 < ITERS:
            residual = residual - step_size * image_out
            norm_next = total_squares(residual)
            direction = residual + norm_next / norm_now * direction
            norm_now = norm_next
    depth_here = solution.shape[0]
    rows_here = solution.shape[1]
    channels = jnp.stack([solution[..., :side_len], solution[..., side_len:]], axis=-1).astype(
        jnp.bfloat16
    )
    first_map = convolve(channels.reshape(depth_here, rows_here, 2 * side_len), conv_in, 2)
    hidden_count = conv_mid.shape[1]
    hidden_one = (
        jax.nn.relu(first_map)
        .astype(jnp.bfloat16)
        .reshape(depth_here, rows_here, side_len * hidden_count)
    )
    second_map = convolve(hidden_one, conv_mid, hidden_count)
    hidden_two = (
        jax.nn.relu(second_map)
        .astype(jnp.bfloat16)
        .reshape(depth_here, rows_here, side_len * hidden_count)
    )
    third_map = convolve(hidden_two, conv_out, hidden_count).reshape(
        depth_here, rows_here, side_len, 2
    )
    refined = solution + jnp.concatenate([third_map[..., 0], third_map[..., 1]], axis=-1)
    return (solution, refined)


def solution(mesh):
    placed = (
        P("slab", "coil", None),
        P("slab", "coil", None),
        P("coil", "slab", None, None),
        P(None, "slab", None),
        P(),
        P(),
        P(),
    )
    return jax.shard_map(
        shards,
        mesh=mesh,
        in_specs=placed,
        out_specs=(P("slab", "coil", None), P("slab", "coil", None)),
        check_vma=False,
    )
```

profile of v0, /device:TPU:249, one launch (start us, length us, event | category | flops | bytes accessed | tf_op | source)
XLA Modules:
  0.0 1028.2 jit_solution(9897725327793448658)
XLA Ops:
  10.4 37.1 %all_gather.6 = f32[1,192,384]{2,0,1:T(1,128)S(1)} all-gather(f32[1,6,384]{2,0,1:T(1,128)S(1)} %copy.111), channel_id=1, replica_groups=mesh['coil'=32,'slab'=16] {'coil'}, dimensions={1}, use_global_device_ids=true | all-gather | bytes 304128 | tf_op jit(solution)/shard_map/all_gather | solution.py:134
  48.9 4.0 convolution_bitcast_fusion.10
  52.9 4.0 convolution_bitcast_fusion.11
  59.8 21.2 %all-to-all-start = ((f32[1,1,384,768]{3,1,0,2:T(1,128)}), f32[1,1,384,768]{3,1,0,2:T(1,128)S(1)}, u32[]{:S(2)}, u32[]{:S(2)}) async-start(f32[1,1,384,768]{3,1,0,2:T(1,128)} %copy.112), calls=%async_computation | async-start | bytes 2359296 | tf_op jit(solution)/shard_map/all_to_all | solution.py:138
  85.1 25.0 %all-to-all-done = f32[1,1,384,768]{3,1,0,2:T(1,128)S(1)} async-done(((f32[1,1,384,768]{3,1,0,2:T(1,128)}), f32[1,1,384,768]{3,1,0,2:T(1,128)S(1)}, u32[]{:S(2)}, u32[]{:S(2)}) %all-to-all-start) | async-done | bytes 1179680 | tf_op jit(solution)/shard_map/all_to_all | solution.py:138
  117.6 5.2 all-to-all-start.1
  127.0 24.9 %all-to-all-done.1 = f32[1,16,24,768]{3,2,0,1:T(8,128)S(1)} async-done(((f32[1,16,24,768]{3,2,0,1:T(8,128)}), f32[1,16,24,768]{3,2,0,1:T(8,128)S(1)}, u32[]{:S(2)}, u32[]{:S(2)}) %all-to-all-start.1) | async-done | bytes 1179680 | tf_op jit(solution)/shard_map/all_to_all | solution.py:144
  162.2 145.9 %all-reduce.9.cloned.1.call-done = f32[1,192,384]{2,0,1:T(1,128)} async-done(((f32[1,192,384]{2,0,1:T(1,128)}), f32[1,192,384]{2,0,1:T(1,128)}) %all-reduce.9.cloned.1.call-update) | async-done | bytes 294928
  309.4 99.0 %all-reduce.5 = (f32[]{:T(128)}, f32[]{:T(128)}) all-reduce(f32[]{:T(128)} %get-tuple-element.13, f32[]{:T(128)} %get-tuple-element.12), channel_id=1, replica_groups=mesh['coil'=32,'slab'=16] {'coil','slab'}, use_global_device_ids=true, to_apply=%region_1.2 | all-reduce | flops 2 | bytes 16 | tf_op jit(solution)/shard_map/psum | solution.py:125
  410.4 94.7 %psum.30 = f32[]{:T(128)} all-reduce(f32[]{:T(128)} %multiply_reduce_fusion), channel_id=1, replica_groups=mesh['coil'=32,'slab'=16] {'coil','slab'}, use_global_device_ids=true, to_apply=%region_6.7 | all-reduce | flops 1 | bytes 8 | tf_op jit(solution)/shard_map/psum | solution.py:125
  506.5 37.2 %all_gather.7 = f32[1,192,384]{2,0,1:T(1,128)S(1)} all-gather(f32[1,6,384]{2,0,1:T(1,128)S(1)} %copy.119), channel_id=1, replica_groups=mesh['coil'=32,'slab'=16] {'coil'}, dimensions={1}, use_global_device_ids=true | all-gather | bytes 304128 | tf_op jit(solution)/shard_map/all_gather | solution.py:134
  545.1 4.0 convolution_bitcast_fusion.8
  556.0 47.3 %all_to_all.16 = f32[1,1,384,768]{3,1,0,2:T(1,128)S(1)} all-to-all(f32[1,1,384,768]{3,1,0,2:T(1,128)} %copy.120), channel_id=1, replica_groups=mesh['coil'=32,'slab'=16] {'slab'}, dimensions={2} | all-to-all | bytes 2359296 | tf_op jit(solution)/shard_map/all_to_all | solution.py:138
  609.9 34.2 %all_to_all.17 = f32[1,16,24,768]{3,2,0,1:T(8,128)S(1)} all-to-all(f32[1,16,24,768]{3,2,0,1:T(8,128)S(1)} %copy.123), channel_id=1, replica_groups=mesh['coil'=32,'slab'=16] {'slab'}, dimensions={1} | all-to-all | bytes 2359296 | tf_op jit(solution)/shard_map/all_to_all | solution.py:144
  652.4 148.8 %all-reduce.11.cloned.1.call-done = f32[1,192,384]{2,0,1:T(1,128)} async-done(((f32[1,192,384]{2,0,1:T(1,128)}), f32[1,192,384]{2,0,1:T(1,128)}) %all-reduce.11.cloned.1.call-update) | async-done | bytes 294928
  802.5 98.9 %psum.31 = f32[]{:T(128)} all-reduce(f32[]{:T(128)} %fusion.74), channel_id=1, replica_groups=mesh['coil'=32,'slab'=16] {'coil','slab'}, use_global_device_ids=true, to_apply=%region_9.10 | all-reduce | flops 1 | bytes 8 | tf_op jit(solution)/shard_map/psum | solution.py:152
  903.1 5.1 collective-permute-start
  910.3 5.3 collective-permute-done.1
  915.8 4.0 collective-permute-start.3
  927.2 4.2 concatenate.143
  947.4 4.0 collective-permute-start.7
  951.4 4.7 collective-permute-start.6
  985.5 4.0 collective-permute-done.9
  992.3 5.5 collective-permute-start.10
  (168 shorter events, 140.2 us)
Async XLA Ops:
  7.2 40.4 %copy-start = (f32[1,1,192,384]{3,2,1,0:T(8,128)S(1)}, f32[1,1,192,384]{3,2,1,0:T(8,128)}, u32[]{:S(2)}) copy-start(f32[1,1,192,384]{3,2,1,0:T(8,128)} %param.9) | copy-start | bytes 884740
  8.3 39.4 %copy-start.5 = (f32[192,384]{1,0:T(8,128)}, f32[192,384]{1,0:T(8,128)S(1)}, u32[]{:S(2)}) copy-start(f32[192,384]{1,0:T(8,128)S(1)} %fusion.66) | copy-start | bytes 884740
  9.5 39.4 %copy-start.7 = (f32[192,384]{1,0:T(8,128)}, f32[192,384]{1,0:T(8,128)S(1)}, u32[]{:S(2)}) copy-start(f32[192,384]{1,0:T(8,128)S(1)} %get-tuple-element.133) | copy-start | bytes 884740
  9.5 39.4 %copy-start.9 = (f32[192,384]{1,0:T(8,128)}, f32[192,384]{1,0:T(8,128)S(1)}, u32[]{:S(2)}) copy-start(f32[192,384]{1,0:T(8,128)S(1)} %get-tuple-element.134) | copy-start | bytes 884740
  59.8 21.2 %copy-start.2 = (f32[16,24,384]{2,1,0:T(8,128)S(1)}, f32[16,24,384]{2,1,0:T(8,128)}, u32[]{:S(2)}) copy-start(f32[16,24,384]{2,1,0:T(8,128)} %param.10) | copy-start | bytes 1769476
  59.8 50.2 %all-to-all-start = ((f32[1,1,384,768]{3,1,0,2:T(1,128)}), f32[1,1,384,768]{3,1,0,2:T(1,128)S(1)}, u32[]{:S(2)}, u32[]{:S(2)}) async-start(f32[1,1,384,768]{3,1,0,2:T(1,128)} %copy.112), calls=%async_computation | async-start | bytes 2359296 | tf_op jit(solution)/shard_map/all_to_all | solution.py:138
  117.6 34.2 %all-to-all-start.1 = ((f32[1,16,24,768]{3,2,0,1:T(8,128)}), f32[1,16,24,768]{3,2,0,1:T(8,128)S(1)}, u32[]{:S(2)}, u32[]{:S(2)}) async-start(f32[1,16,24,768]{3,2,0,1:T(8,128)} %copy.116), calls=%async_computation.1 | async-start | bytes 2359296 | tf_op jit(solution)/shard_map/all_to_all | solution.py:144
  122.8 185.3 %all-reduce.9.cloned.1.call-start = ((), (), s32[]{:S(2)}) async-start(), calls=%async_computation.4 | async-start | bytes 589824
  160.1 383.8 %copy-start.6 = (f32[192,384]{1,0:T(8,128)S(1)}, f32[192,384]{1,0:T(8,128)}, u32[]{:S(2)}) copy-start(f32[192,384]{1,0:T(8,128)} %copy-done.5) | copy-start | bytes 884740
  160.1 383.8 %copy-start.8 = (f32[192,384]{1,0:T(8,128)S(1)}, f32[192,384]{1,0:T(8,128)}, u32[]{:S(2)}) copy-start(f32[192,384]{1,0:T(8,128)} %copy-done.7) | copy-start | bytes 884740
  160.2 383.8 %copy-start.10 = (f32[192,384]{1,0:T(8,128)S(1)}, f32[192,384]{1,0:T(8,128)}, u32[]{:S(2)}) copy-start(f32[192,384]{1,0:T(8,128)} %copy-done.9) | copy-start | bytes 884740
  160.2 641.0 %all-reduce.11.cloned.1.call-start = ((), (), s32[]{:S(2)}) async-start(), calls=%async_computation.5 | async-start | bytes 589824
  903.1 7.1 collective-permute-start
  908.2 7.5 collective-permute-start.1
  915.8 7.5 collective-permute-start.3
  919.8 4.0 collective-permute-start.2
  938.3 5.3 collective-permute-start.4
  940.3 6.9 collective-permute-start.5
  947.4 9.9 collective-permute-start.7
  951.4 7.1 collective-permute-start.6
  980.2 5.3 collective-permute-start.8
  982.1 7.4 collective-permute-start.9
  989.6 9.7 collective-permute-start.11
  992.3 8.1 collective-permute-start.10
  (5 other events, 8.6 us)
Sparse Core Ops, SparseCore 0:
  160.3 147.8 all-reduce.8
  652.5 148.5 all-reduce.10
where the time goes:
time: 1030 us
  blocking collectives  449 us (44%)
  waiting for transfers between devices  362 us (35%)
  starting transfers between devices  68.6 us (7%)
  local copies, waits for them, and re-layouts  64.6 us (6%)
  matrix products  52.4 us (5%)
  between operations  19.8 us (2%)
  other arithmetic  12 us (1%)
    unnamed x4, waiting for transfers between devices  295 us
    psum x2, blocking collectives, total_squares(): return lax.psum(jnp.sum(residual * residual), ('coil', 'slab'))  194 us
    psum x1, blocking collectives, shards(): curvature = lax.psum(local_curv, ('coil', 'slab'))  98.9 us
    all_gather x2, blocking collectives, shards(): lax.all_gather(direction, 'coil', axis=1, tiled=True)[None]  74.3 us
    all_to_all x1, blocking collectives, shards(): lax.all_to_all(spread, 'slab', split_axis=2, concat_axis=1, tiled=True)  47.3 us
    all_to_all x1, blocking collectives, shards(): lax.all_to_all(returned, 'slab', split_axis=1, concat_axis=2, tiled=True)  34.2 us
    concatenate x12, local copies, waits for them, and re-layouts, convolve(): patches = jnp.concatenate(tap_list, axis=-1).reshape(-1, width_taps)  26.8 us
    all_to_all x1, waiting for transfers between devices, shards(): lax.all_to_all(spread, 'slab', split_axis=2, concat_axis=1, tiled=True)  25 us
  transfers between devices with their start and end apart: 16, of which 12 were waited for; matrix products, arithmetic and copies ran while one was open for 1% of the time, Pallas kernels for 0%

commit v1 on v0

--- a/solution.py
+++ b/solution.py
@@ -3,6 +3,7 @@
 import jax.numpy as jnp
 from jax import lax
 from jax.sharding import PartitionSpec as P
+from jax.lax import all_to_all, axis_size
 
 ITERS = 2
 reg_weight = 0.5
@@ -135,7 +136,12 @@
         )
         products = jnp.matmul(products, fwd_last, precision=highest)
         spread = along_axis(products, fwd_plane, "kn,cznw->czkw")
-        apply_pencil = lax.all_to_all(spread, "slab", split_axis=2, concat_axis=1, tiled=True)
+        apply_pencil = jnp.concatenate(
+            all_to_all(
+                jnp.stack(jnp.split(spread, axis_size("slab"), axis=2), axis=0), "slab", 0, 0
+            ),
+            axis=1,
+        )
         spectrum = along_axis(apply_pencil, fwd_depth, "kn,cnxw->ckxw")
         shape_now = spectrum.shape
         split_form = spectrum.reshape(shape_now[0], shape_now[1], shape_now[2], 2, grid_len)

time: 1030 us -> 1080 us (1.049)
  local copies, waits for them, and re-layouts: 64.6 us -> 106 us
    another operation x0 -> x34, local copies, waits for them, and re-layouts: none -> 36.5 us  [shards(): jnp.stack(jnp.split(spread, axis_size('slab'), axis=2), axis=0)]
    unnamed x36 -> x132, local copies, waits for them, and re-layouts: 6.16 us -> 17.3 us
where the time goes in v1:
time: 1080 us
  blocking collectives  448 us (41%)
  waiting for transfers between devices  362 us (34%)
  local copies, waits for them, and re-layouts  106 us (10%)
  starting transfers between devices  68.1 us (6%)
  matrix products  52.7 us (5%)
  between operations  20.1 us (2%)
  other arithmetic  20 us (2%)
    unnamed x4, waiting for transfers between devices  295 us
    psum x2, blocking collectives, total_squares(): return lax.psum(jnp.sum(residual * residual), ('coil', 'slab'))  194 us
    psum x1, blocking collectives, shards(): curvature = lax.psum(local_curv, ('coil', 'slab'))  99 us
    all_gather x2, blocking collectives, shards(): lax.all_gather(direction, 'coil', axis=1, tiled=True)[None]  74.3 us
    all_to_all x1, blocking collectives, shards(): all_to_all(jnp.stack(jnp.split(spread, axis_size('slab'), axis=2), axis=0...  46.5 us
    another operation x34, local copies, waits for them, and re-layouts, shards(): jnp.stack(jnp.split(spread, axis_size('slab'), axis=2), axis=0)  36.5 us
    all_to_all x1, blocking collectives, shards(): lax.all_to_all(returned, 'slab', split_axis=1, concat_axis=2, tiled=True)  34.4 us
    concatenate x12, local copies, waits for them, and re-layouts, convolve(): patches = jnp.concatenate(tap_list, axis=-1).reshape(-1, width_taps)  26.1 us
  transfers between devices with their start and end apart: 16, of which 12 were waited for; matrix products, arithmetic and copies ran while one was open for 1% of the time, Pallas kernels for 0%

profile of v1, /device:TPU:249, one launch (start us, length us, event | category | flops | bytes accessed | tf_op | source)
XLA Modules:
  0.0 1077.3 jit_solution(4605016260307838351)
XLA Ops:
  10.4 37.1 %all_gather.6 = f32[1,192,384]{2,0,1:T(1,128)S(1)} all-gather(f32[1,6,384]{2,0,1:T(1,128)S(1)} %copy.135), channel_id=1, replica_groups=mesh['coil'=32,'slab'=16] {'coil'}, dimensions={1}, use_global_device_ids=true | all-gather | bytes 304128 | tf_op jit(solution)/shard_map/all_gather | solution.py:135
  48.9 4.0 convolution_bitcast_fusion.10
  52.9 4.0 convolution_bitcast_fusion.11
  86.8 20.6 %all-to-all-start = ((f32[16,1,1,24,768]{4,3,2,1,0:T(8,128)}), f32[16,1,1,24,768]{4,3,2,1,0:T(8,128)S(1)}, u32[]{:S(2)}, u32[]{:S(2)}) async-start(f32[16,1,1,24,768]{4,3,2,1,0:T(8,128)} %constant_dynamic-update-slice_fusion), calls=%async_computation | async-start | bytes 2359296 | tf_op jit(solution)/shard_map/all_to_all | solution.py:140
  111.5 25.0 %all-to-all-done = f32[16,1,1,24,768]{4,3,2,1,0:T(8,128)S(1)} async-done(((f32[16,1,1,24,768]{4,3,2,1,0:T(8,128)}), f32[16,1,1,24,768]{4,3,2,1,0:T(8,128)S(1)}, u32[]{:S(2)}, u32[]{:S(2)}) %all-to-all-start) | async-done | bytes 1179680 | tf_op jit(solution)/shard_map/all_to_all | solution.py:140
  143.9 5.2 all-to-all-start.1
  153.3 24.8 %all-to-all-done.1 = f32[1,16,24,768]{3,2,0,1:T(8,128)S(1)} async-done(((f32[1,16,24,768]{3,2,0,1:T(8,128)}), f32[1,16,24,768]{3,2,0,1:T(8,128)S(1)}, u32[]{:S(2)}, u32[]{:S(2)}) %all-to-all-start.1) | async-done | bytes 1179680 | tf_op jit(solution)/shard_map/all_to_all | solution.py:150
  188.6 145.9 %all-reduce.9.cloned.1.call-done = f32[1,192,384]{2,0,1:T(1,128)} async-done(((f32[1,192,384]{2,0,1:T(1,128)}), f32[1,192,384]{2,0,1:T(1,128)}) %all-reduce.9.cloned.1.call-update) | async-done | bytes 294928
  335.8 99.0 %all-reduce.5 = (f32[]{:T(128)}, f32[]{:T(128)}) all-reduce(f32[]{:T(128)} %get-tuple-element.13, f32[]{:T(128)} %get-tuple-element.12), channel_id=1, replica_groups=mesh['coil'=32,'slab'=16] {'coil','slab'}, use_global_device_ids=true, to_apply=%region_1.2 | all-reduce | flops 2 | bytes 16 | tf_op jit(solution)/shard_map/psum | solution.py:126
  436.8 94.7 %psum.30 = f32[]{:T(128)} all-reduce(f32[]{:T(128)} %multiply_reduce_fusion), channel_id=1, replica_groups=mesh['coil'=32,'slab'=16] {'coil','slab'}, use_global_device_ids=true, to_apply=%region_6.7 | all-reduce | flops 1 | bytes 8 | tf_op jit(solution)/shard_map/psum | solution.py:126
  532.9 37.2 %all_gather.7 = f32[1,192,384]{2,0,1:T(1,128)S(1)} all-gather(f32[1,6,384]{2,0,1:T(1,128)S(1)} %copy.157), channel_id=1, replica_groups=mesh['coil'=32,'slab'=16] {'coil'}, dimensions={1}, use_global_device_ids=true | all-gather | bytes 304128 | tf_op jit(solution)/shard_map/all_gather | solution.py:135
  571.5 4.0 convolution_bitcast_fusion.8
  605.4 46.5 %all_to_all.28 = f32[16,1,1,24,768]{4,3,2,1,0:T(8,128)S(1)} all-to-all(f32[16,1,1,24,768]{4,3,2,1,0:T(8,128)S(1)} %constant_dynamic-update-slice_fusion.16), channel_id=1, replica_groups=mesh['coil'=32,'slab'=16] {'slab'}, dimensions={0} | all-to-all | bytes 2359296 | tf_op jit(solution)/shard_map/all_to_all | solution.py:140
  658.3 34.4 %all_to_all.29 = f32[1,16,24,768]{3,2,0,1:T(8,128)S(1)} all-to-all(f32[1,16,24,768]{3,2,0,1:T(8,128)S(1)} %copy.175), channel_id=1, replica_groups=mesh['coil'=32,'slab'=16] {'slab'}, dimensions={1} | all-to-all | bytes 2359296 | tf_op jit(solution)/shard_map/all_to_all | solution.py:150
  701.4 148.8 %all-reduce.11.cloned.1.call-done = f32[1,192,384]{2,0,1:T(1,128)} async-done(((f32[1,192,384]{2,0,1:T(1,128)}), f32[1,192,384]{2,0,1:T(1,128)}) %all-reduce.11.cloned.1.call-update) | async-done | bytes 294928
  851.4 99.0 %psum.31 = f32[]{:T(128)} all-reduce(f32[]{:T(128)} %fusion.140), channel_id=1, replica_groups=mesh['coil'=32,'slab'=16] {'coil','slab'}, use_global_device_ids=true, to_apply=%region_9.10 | all-reduce | flops 1 | bytes 8 | tf_op jit(solution)/shard_map/psum | solution.py:158
  952.1 5.1 collective-permute-start
  959.3 5.3 collective-permute-done.1
  964.8 4.0 collective-permute-start.3
  976.2 4.2 concatenate.143
  996.6 4.0 collective-permute-start.7
  1000.7 4.7 collective-permute-start.6
  1034.7 4.0 collective-permute-done.9
  1041.6 5.5 collective-permute-start.10
  (298 shorter events, 190.1 us)
Async XLA Ops:
  7.2 40.4 %copy-start = (f32[1,1,192,384]{3,2,1,0:T(8,128)S(1)}, f32[1,1,192,384]{3,2,1,0:T(8,128)}, u32[]{:S(2)}) copy-start(f32[1,1,192,384]{3,2,1,0:T(8,128)} %param.9) | copy-start | bytes 884740
  8.3 39.4 %copy-start.40 = (f32[192,384]{1,0:T(8,128)}, f32[192,384]{1,0:T(8,128)S(1)}, u32[]{:S(2)}) copy-start(f32[192,384]{1,0:T(8,128)S(1)} %fusion.132) | copy-start | bytes 884740
  9.5 39.4 %copy-start.42 = (f32[192,384]{1,0:T(8,128)}, f32[192,384]{1,0:T(8,128)S(1)}, u32[]{:S(2)}) copy-start(f32[192,384]{1,0:T(8,128)S(1)} %get-tuple-element.165) | copy-start | bytes 884740
  9.5 39.4 %copy-start.44 = (f32[192,384]{1,0:T(8,128)}, f32[192,384]{1,0:T(8,128)S(1)}, u32[]{:S(2)}) copy-start(f32[192,384]{1,0:T(8,128)S(1)} %get-tuple-element.166) | copy-start | bytes 884740
  86.8 49.6 %all-to-all-start = ((f32[16,1,1,24,768]{4,3,2,1,0:T(8,128)}), f32[16,1,1,24,768]{4,3,2,1,0:T(8,128)S(1)}, u32[]{:S(2)}, u32[]{:S(2)}) async-start(f32[16,1,1,24,768]{4,3,2,1,0:T(8,128)} %constant_dynamic-update-slice_fusion), calls=%async_computation | async-start | bytes 2359296 | tf_op jit(solution)/shard_map/all_to_all | solution.py:140
  143.9 34.2 %all-to-all-start.1 = ((f32[1,16,24,768]{3,2,0,1:T(8,128)}), f32[1,16,24,768]{3,2,0,1:T(8,128)S(1)}, u32[]{:S(2)}, u32[]{:S(2)}) async-start(f32[1,16,24,768]{3,2,0,1:T(8,128)} %copy.154), calls=%async_computation.1 | async-start | bytes 2359296 | tf_op jit(solution)/shard_map/all_to_all | solution.py:150
  149.2 185.4 %all-reduce.9.cloned.1.call-start = ((), (), s32[]{:S(2)}) async-start(), calls=%async_computation.4 | async-start | bytes 589824
  150.9 32.0 %copy-start.15 = (f32[384,192]{1,0:T(8,128)}, f32[384,192]{1,0:T(8,128)S(1)}, u32[]{:S(2)}) copy-start(f32[384,192]{1,0:T(8,128)S(1)} %fusion.125) | copy-start | bytes 884740
  186.5 383.8 %copy-start.41 = (f32[192,384]{1,0:T(8,128)S(1)}, f32[192,384]{1,0:T(8,128)}, u32[]{:S(2)}) copy-start(f32[192,384]{1,0:T(8,128)} %copy-done.40) | copy-start | bytes 884740
  186.5 383.8 %copy-start.43 = (f32[192,384]{1,0:T(8,128)S(1)}, f32[192,384]{1,0:T(8,128)}, u32[]{:S(2)}) copy-start(f32[192,384]{1,0:T(8,128)} %copy-done.42) | copy-start | bytes 884740
  186.5 383.8 %copy-start.45 = (f32[192,384]{1,0:T(8,128)S(1)}, f32[192,384]{1,0:T(8,128)}, u32[]{:S(2)}) copy-start(f32[192,384]{1,0:T(8,128)} %copy-done.44) | copy-start | bytes 884740
  186.5 663.6 %all-reduce.11.cloned.1.call-start = ((), (), s32[]{:S(2)}) async-start(), calls=%async_computation.5 | async-start | bytes 589824
  952.1 7.1 collective-permute-start
  957.2 7.5 collective-permute-start.1
  964.8 7.5 collective-permute-start.3
  968.8 4.0 collective-permute-start.2
  987.6 5.3 collective-permute-start.4
  989.5 6.9 collective-permute-start.5
  996.6 9.9 collective-permute-start.7
  1000.7 7.1 collective-permute-start.6
  1029.4 5.3 collective-permute-start.8
  1031.3 7.4 collective-permute-start.9
  1038.8 9.7 collective-permute-start.11
  1041.6 8.1 collective-permute-start.10
  (39 other events, 143.5 us)
Sparse Core Ops, SparseCore 0:
  186.6 147.8 all-reduce.8
  701.5 148.6 all-reduce.10
